TPU v7x, 128 devices: a whole 4x4x4 slice. The times are simulated.
128 devices in a mesh: gx: 8 (over x_lo, z), gy: 8 (over y, core), gz: 2 (over x_hi).
Axes of the slice: x: 4 (x_hi: 2, x_lo: 2; x = x_hi * 2 + x_lo), y: 4, z: 4, core: 2. Of those that a mesh axis runs over, the one named last changes fastest.
Arguments:
- basis: bfloat16 [64, 64, 16, 8192], P('gx', 'gy', 'gz'), may hold values from -0.09375 to 0.09375
- classes: int32 [64, 64, 16], P('gx', 'gy', 'gz'), may hold values from 0 to 15
- cond_table: float32 [16], replicated, may hold values from 0.5 to 2
- ground_table: float32 [16], replicated, may hold values from 4 to 40
- port_cells: int32 [2048], replicated, may hold values from 0 to 65535
- port_load: float32 [2048], replicated, may hold values from 20 to 200
Outputs:
- reduced: float32 [8192, 1024], P(('gx', 'gz'), 'gy')
- factor: float32 [8192, 1024], P(('gx', 'gz'), 'gy')
Inputs may be any that keep to these rules, and one draw needn't show every extreme that they name: `port_cells`: several ports may name the same cell; their loads add.
All inputs are finite; a program needn't handle non-finite values.
Results may differ from a plain program's by a relative error of at most 0.0024.
Values may be sent and summed in bfloat16 or wider, within the bound.
A program may use at most 256 MiB of HBM per device.

v0:
```python
import jax
import jax.numpy as jnp
from jax import lax
from jax.experimental import pallas as pl
from jax.experimental.pallas import tpu as pltpu
from jax.sharding import PartitionSpec as P

NB = 512
PANELS = 2
COLS = NB * PANELS
F32 = jnp.float32
BF16 = jnp.bfloat16
MESH = pl.DeviceIdType.MESH


def here():
    gx, gy, gz = lax.axis_index("gx"), lax.axis_index("gy"), lax.axis_index("gz")
    return gz * 2 + gx // 4, gy // 2, gx % 4, gy % 2


def device(x, y, z, core):
    return ((x % 2) * 4 + z, y * 2 + core, x // 2)


def along(axis, pos, place):
    x, y, z, core = place
    if axis == "x":
        x = pos
    elif axis == "y":
        y = pos
    else:
        z = pos
    return device(x, y, z, core)


def position(axis, place):
    return place["xyz".index(axis)]


def greet(devices):
    barrier = pltpu.get_barrier_semaphore()
    for dev in devices:
        pl.semaphore_signal(barrier, inc=1, device_id=dev, device_id_type=MESH)
    pl.semaphore_wait(barrier, len(devices))


def torus_peers(place):
    x, y, z, core = place
    peers = []
    for axis in "xyz":
        pos = position(axis, place)
        peers += [along(axis, (pos + 1) % 4, place), along(axis, (pos + 3) % 4, place)]
    return peers + [device(x, y, z, 1 - core)]


class Wires:
    def __init__(self, send_sem, recv_sem):
        self.send_sem, self.recv_sem, self.used = send_sem, recv_sem, 0

    def take(self, count=1):
        self.used += count
        return self.used - count

    def copy(self, number, src, dst, dev):
        return pltpu.make_async_remote_copy(
            src_ref=src,
            dst_ref=dst,
            send_sem=self.send_sem.at[number],
            recv_sem=self.recv_sem.at[number],
            device_id=dev,
            device_id_type=MESH,
        )

    def send(self, number, src, dst, dev):
        copy = self.copy(number, src, dst, dev)
        copy.start()
        return copy


def each(dims, body):
    count = 4 ** len(dims)
    if count == 1:
        body(())
        return

    def step(i, _):
        body(tuple((i // 4 ** (len(dims) - 1 - d)) % 4 for d in range(len(dims))))
        return 0

    lax.fori_loop(0, count, step, 0)


def put(index, dims, axis, pos):
    index = list(index)
    index.insert(dims.index(axis), pos)
    return tuple(index)


class Reduce:
    def __init__(self, place, wires, axis, dims, home, out, rows, lane, got):
        self.axis, self.dims, self.home, self.out, self.rows, self.got = axis, dims, home, out, rows, got
        self.first, self.second = pl.ds(lane, 128), pl.ds(lane + 128, 128)
        self.rest = tuple(d for d in dims if d != axis)
        self.wires, self.base = wires, wires.take(6)
        me = position(axis, place)
        self.me, self.plus, self.minus, self.opposite = me, (me + 1) % 4, (me + 3) % 4, (me + 2) % 4
        self.up, self.down = along(axis, self.plus, place), along(axis, self.minus, place)
        self.copies = {}

    def go(self, slot, pos, lanes, dev):
        index = put([pl.ds(0, 4)] * len(self.rest), self.dims, self.axis, pos)
        src = self.out.at[index + (self.rows, lanes)]
        self.copies[slot] = self.wires.send(self.base + slot, src, self.got.at[slot], dev)

    def begin(self):
        self.go(0, self.opposite, self.first, self.up)
        self.go(3, self.opposite, self.second, self.down)

    def follow(self):
        self.go(1, self.plus, self.second, self.up)
        self.go(4, self.minus, self.first, self.down)

    def relay(self):
        for slot, pos, lanes, dev in (
            (0, self.plus, self.first, self.up),
            (3, self.minus, self.second, self.down),
        ):
            self.copies[slot].wait_recv()

            def body(index):
                at = put(index, self.dims, self.axis, pos) + (self.rows, lanes)
                total = self.home[at] + self.got[(slot,) + index].astype(F32)
                self.out[at] = total.astype(self.out.dtype)

            each(self.rest, body)
            self.go(slot + 2, pos, lanes, dev)

    def finish(self, store):
        for slot in (1, 4, 2, 5):
            self.copies[slot].wait_recv()

        def body(index):
            for half, lanes, one, two in ((0, self.first, 2, 4), (1, self.second, 1, 5)):
                at = put(index, self.dims, self.axis, self.me) + (self.rows, lanes)
                total = self.home[at] + self.got[(one,) + index].astype(F32)
                store(index, half, total + self.got[(two,) + index].astype(F32))

        each(self.rest, body)
        for copy in self.copies.values():
            copy.wait_send()


class Gather:
    def __init__(self, place, wires, axis, ref, base, size, lanes, halves, mate=None):
        self.ref, self.base, self.size, self.mate = ref, base, size, mate
        self.lanes, self.halves = lanes, halves
        self.wires, self.first = wires, wires.take(8)
        me = position(axis, place)
        self.me, self.plus, self.minus, self.opposite = me, (me + 1) % 4, (me + 3) % 4, (me + 2) % 4
        self.up, self.down = along(axis, self.plus, place), along(axis, self.minus, place)
        self.copies = []
        self.passed = []

    def go(self, slot, pos, lanes, dev):
        rows = pl.ds(pl.multiple_of(self.base + pos * self.size, self.size), self.size)
        part = self.ref.at[rows, lanes]
        return self.wires.send(self.first + slot, part, part, dev)

    def share(self, slot, pos):
        if self.mate is not None:
            self.passed.append(self.go(slot, pos, self.lanes, self.mate))

    def begin(self):
        self.copies += [self.go(0, self.me, self.lanes, self.up)]
        self.copies += [self.go(1, self.me, self.lanes, self.down)]
        self.share(4, self.me)

    def relay(self):
        self.copies[0].wait_recv()
        self.copies += [self.go(2, self.minus, self.halves[0], self.up)]
        self.copies[1].wait_recv()
        self.copies += [self.go(3, self.plus, self.halves[1], self.down)]
        self.share(5, self.minus)
        self.share(6, self.plus)

    def arrive(self):
        self.copies[2].wait_recv()
        self.copies[3].wait_recv()
        self.share(7, self.opposite)

    def finish(self):
        for copy in self.passed:
            copy.wait_recv()
        for copy in self.copies + self.passed:
            copy.wait_send()


def row_of(block, k):
    return jnp.broadcast_to(block[k : k + 1, :], block.shape)


def pieces(value, count):
    terms = []
    for _ in range(count):
        term = value.astype(BF16).astype(F32)
        terms.append(term)
        value = value - term
    return terms


def eliminate(rows, right, cols, sub):
    scale = jnp.zeros((8, 128), F32)
    for k in range(8):
        inv = 1.0 / row_of(cols[0][k], k)
        scale = jnp.where(sub == k, inv, scale)
        pivot_row = row_of(rows[0], k)
        pivot_right = row_of(right[0], k)
        heads = [row_of(cols[0][m], k) for m in range(k + 1, 8)]
        for t in range(len(rows)):
            mult = cols[t][k] * inv
            if t == 0:
                mult = jnp.where(sub > k, mult, 0.0)
            for i, m in enumerate(range(k + 1, 8)):
                cols[t][m] = cols[t][m] - mult * heads[i]
            rows[t] = rows[t] - mult * pivot_row
            right[t] = right[t] - mult * pivot_right
    return rows, right, scale


def stack_dot(left, right):
    a1, a2, a3 = pieces(left, 3)
    b1, b2, b3 = pieces(right, 3)
    a = jnp.concatenate([a1, a1, a2, a2, a1, a3], axis=0).astype(BF16)
    b = jnp.concatenate([b1, b2, b1, b2, b3, b1], axis=0).astype(BF16)
    return lax.dot_general(a, b, (((0,), (0,)), ((), ())), preferred_element_type=F32)


def factor_block(a_ref, x_ref, middle):
    sub = lax.broadcasted_iota(jnp.int32, (8, 128), 0)
    row = lax.broadcasted_iota(jnp.int32, (128, 128), 0)
    lane = lax.broadcasted_iota(jnp.int32, (128, 128), 1)
    x_ref[...] = jnp.where(row == lane, 1.0, 0.0).astype(F32)
    for g in range(16):
        b = g * 8
        n = 2 if g < 15 else 1
        rows = [a_ref[b + 8 * t : b + 8 * t + 8, :] for t in range(n)]
        right = [x_ref[b + 8 * t : b + 8 * t + 8, :] for t in range(n)]
        cols = [
            [jnp.broadcast_to(rows[t][:, b + m : b + m + 1], (8, 128)) for m in range(8)]
            for t in range(n)
        ]
        rows, right, scale = eliminate(rows, right, cols, sub)
        if n == 2:
            a_ref[b + 8 : b + 16, :] = rows[1]
            x_ref[b + 8 : b + 16, :] = right[1]
        if g < 14:
            low = b + 16
            both = jnp.concatenate([rows[0], right[0]], axis=1)
            change = stack_dot(rows[0] * scale, both)
            a_ref[low:, :] = a_ref[low:, :] - change[low:, :128]
            x_ref[low:, :] = x_ref[low:, :] - change[low:, 128:]
        x_ref[b : b + 8, :] = right[0] * jnp.sqrt(scale)
        middle(g)


def two(value):
    high = value.astype(BF16)
    return high, (value - high.astype(F32)).astype(BF16)


def dot_two(left, right):
    lh, ll = two(left)
    rh, rl = two(right)
    return jnp.dot(
        jnp.concatenate([lh, ll, lh], axis=1),
        jnp.concatenate([rh, rh, rl], axis=0),
        preferred_element_type=F32,
    )


def invert_factor(work, a_ref, x_ref, between):
    n = work.shape[0]
    for k in range(n // 128):
        b, e = k * 128, k * 128 + 128
        a_ref[...] = work[b:e, b:e]
        factor_block(a_ref, x_ref, between)
        inverse = x_ref[...]
        for low, high in ((0, b), (e, n)):
            if low < high:
                work[b:e, low:high] = dot_two(inverse, work[b:e, low:high])
        work[b:e, b:e] = inverse
        if e < n:
            high, low = two(work[b:e, :])
            left = jnp.concatenate([high[:, e:], low[:, e:], high[:, e:]], axis=0)
            both = jnp.concatenate([high, high, low], axis=0)
            change = lax.dot_general(
                left, both, (((0,), (0,)), ((), ())), preferred_element_type=F32
            )
            if b:
                work[e:, :b] = work[e:, :b] - change[:, :b]
            work[e:, b:e] = -change[:, b:e]
            work[e:, e:] = work[e:, e:] - change[:, e:]
        between(16)


DIMS = "xzy"
ORDERS = ("xyz", "yzx", "zxy")
LEAD_ORDERS = ("xyz", "yzx")
PARTS = ((0, 96), (96, 80), (176, 80))
EVERY = slice(None)
CHUNKS = COLS // 128


def kernel(
    basis, cond, ground, tile, factor, other,
    panel, scaled, faces, halos, hz, image, image_t,
    lead_window, lead_home, lead_out, window, home, out, work, a_ref, x_ref, total, rows_t,
    *rest,
):
    lead_gots, lead_sums, gots, sums = rest[:6], rest[6:10], rest[10:19], rest[19:25]
    load_sem, send_sem, recv_sem = rest[25:]
    wires = Wires(send_sem, recv_sem)
    gx, gy, gz = lax.axis_index("gx"), lax.axis_index("gy"), lax.axis_index("gz")
    place = here()
    x, y, z, core = place
    mate = device(x, y, z, 1 - core)
    beside = [
        ((gx + 7) % 8, gy, gz),
        ((gx + 1) % 8, gy, gz),
        (gx, (gy + 7) % 8, gz),
        (gx, (gy + 1) % 8, gz),
        (gx, gy, 1 - gz),
    ]
    load = pltpu.make_async_copy(basis.at[:, pl.ds(0, COLS)], panel, load_sem.at[0])
    load.start()
    own_lead = []
    for rb in range(2):
        begin = pl.multiple_of(rb * 512 + core * 256, 256)
        own_lead.append(
            pltpu.make_async_copy(
                basis.at[:, pl.ds(begin, 256)],
                lead_window.at[pl.ds(0, 512), pl.ds(rb * 256, 256)],
                load_sem.at[1 + rb],
            )
        )
        own_lead[rb].start()
    greet(beside + torus_peers(place))

    swap_base = wires.take(16)

    def swap(rb, dst):
        begin = pl.multiple_of(rb * 512 + (1 - core) * 256, 256)
        return wires.copy(swap_base + rb, basis.at[:, pl.ds(begin, 256)], dst, mate)

    def far(rb):
        return other.at[:, pl.ds(pl.multiple_of(rb * 256, 256), 256)]

    lead_swaps = [
        swap(rb, lead_window.at[pl.ds(512, 512), pl.ds(rb * 256, 256)]) for rb in range(2)
    ]
    for copy in lead_swaps:
        copy.start()
    load.wait()

    def scale(c, _):
        lanes = pl.ds(pl.multiple_of(c * 128, 128), 128)
        inner = lax.broadcasted_iota(jnp.int32, (8, 128), 0)
        y_low, y_high, z_face = [], [], []
        for i in range(8):
            rows = pl.ds(i * 64, 64)
            value = (cond[rows, :] * panel[rows, lanes].astype(F32)).astype(BF16)
            scaled[rows, lanes] = value
            if i == 0:
                faces[0, :, lanes] = value
            if i == 7:
                faces[1, :, lanes] = value
            value = value.astype(F32)
            y_low.append(value[:8])
            y_high.append(value[56:])
            face = jnp.zeros((8, 128), F32)
            for j in range(8):
                cell = value[j * 8 : j * 8 + 8]
                low = jnp.broadcast_to(cell[0:1, :], (8, 128))
                high = jnp.broadcast_to(cell[7:8, :], (8, 128))
                face = jnp.where(inner == j, jnp.where(gz == 1, low, high), face)
            z_face.append(face)
        for f, face in ((2, y_low), (3, y_high), (4, z_face)):
            faces[f, :, lanes] = jnp.concatenate(face, axis=0).astype(BF16)
        return 0

    lax.fori_loop(0, CHUNKS, scale, 0)
    lands = [1, 0, 3, 2, 4]
    face_base = wires.take(5)
    face_copies = [
        wires.send(face_base + f, faces.at[f], halos.at[lands[f]], beside[f]) for f in range(5)
    ]

    def start_swap(rb, _):
        swap(rb, far(rb)).start()
        return 0

    lax.fori_loop(2, 16, start_swap, 0)
    for copy in face_copies:
        copy.wait()

    keep = [gx > 0, gx < 7, gy > 0, gy < 7]
    image_base = wires.take(CHUNKS)

    def image_copy(c):
        lanes = pl.ds(pl.multiple_of(c * 128, 128), 128)
        return wires.copy(
            image_base + c, image.at[pl.ds(0, 512), lanes], image.at[pl.ds(512, 512), lanes], mate
        )

    def stencil(c, _):
        lanes = pl.ds(pl.multiple_of(c * 128, 128), 128)
        inner = lax.broadcasted_iota(jnp.int32, (64, 128), 0) % 8

        def halo(f):
            return jnp.where(keep[f], halos[f, :, lanes].astype(F32), 0.0)

        hz[...] = halos[4, :, lanes].astype(F32)
        x_low, x_high, y_low, y_high = halo(0), halo(1), halo(2), halo(3)
        for i in range(8):
            rows = pl.ds(i * 64, 64)
            me = scaled[rows, lanes].astype(F32)
            down = scaled[pl.ds((i - 1) * 64, 64), lanes].astype(F32) if i > 0 else x_low
            up = scaled[pl.ds((i + 1) * 64, 64), lanes].astype(F32) if i < 7 else x_high
            around = up + down
            around = around + jnp.concatenate([me[8:], y_high[i * 8 : i * 8 + 8]], axis=0)
            around = around + jnp.concatenate([y_low[i * 8 : i * 8 + 8], me[:56]], axis=0)
            ends = jnp.concatenate(
                [jnp.broadcast_to(hz[i * 8 + j : i * 8 + j + 1, :], (8, 128)) for j in range(8)],
                axis=0,
            )
            high = pltpu.roll(me, 63, 0)
            low = pltpu.roll(me, 1, 0)
            high = jnp.where(inner == 7, jnp.where(gz == 0, ends, 0.0), high)
            low = jnp.where(inner == 0, jnp.where(gz == 1, ends, 0.0), low)
            around = around + high + low
            value = cond[rows, :] * (6.0 * me - around)
            value = value + ground[rows, :] * panel[rows, lanes].astype(F32)
            image[rows, lanes] = value.astype(BF16)
        image_copy(c).start()
        return 0

    lax.fori_loop(0, CHUNKS, stencil, 0)

    def turn(c, _):
        image_copy(c).wait()
        rows = pl.ds(pl.multiple_of(c * 128, 128), 128)
        image_t[rows, :] = image[:, rows].T
        return 0

    lax.fori_loop(0, CHUNKS, turn, 0)

    for copy in own_lead + lead_swaps:
        copy.wait()

    def lead_terms(c, _):
        rows = pl.ds(pl.multiple_of(c * 256, 256), 256)
        product = jnp.dot(image_t[rows, :], lead_window[...], preferred_element_type=F32)
        for i in range(16):
            value = product[i * 16 : i * 16 + 16, :]
            lead_home[c, i // 4, i % 4] = value
            lead_out[c, i // 4, i % 4] = value.astype(BF16)
        return 0

    lax.fori_loop(0, 4, lead_terms, 0)

    def fetch(rb):
        slot = rb % 2
        begin = pl.multiple_of(rb * 512 + core * 256, 256)
        return (
            pltpu.make_async_copy(
                basis.at[:, pl.ds(begin, 256)],
                window.at[slot, pl.ds(0, 512), :],
                load_sem.at[3 + slot],
            ),
            pltpu.make_async_copy(
                far(rb), window.at[slot, pl.ds(512, 512), :], load_sem.at[5 + slot]
            ),
        )

    def start_fetch(rb):
        swap(rb, far(rb)).wait()
        for copy in fetch(rb):
            copy.start()

    def multiply(rb, read):
        to_x, to_z = (rb % 2) * 2 + rb // 8, (rb // 2) % 4

        def one(c, _):
            rows = pl.ds(pl.multiple_of(c * 256, 256), 256)
            product = jnp.dot(image_t[rows, :], read(), preferred_element_type=F32)
            home[to_x, to_z, c] = product
            out[to_x, to_z, c] = product.astype(BF16)
            return 0

        lax.fori_loop(0, 4, one, 0)

    def terms(low, high):
        def one(rb, _):
            for copy in fetch(rb):
                copy.wait()

            @pl.when(rb < 15)
            def _():
                start_fetch(rb + 1)

            multiply(rb, lambda: window[rb % 2])
            return 0

        lax.fori_loop(low, high, one, 0)

    def lead_block(rb):
        multiply(rb, lambda: lead_window[:, rb * 256 : rb * 256 + 256])

    dims = [LEAD_ORDERS[p] for p in range(2)]
    homes, outs, lane = [lead_home] * 2, [lead_out] * 2, [0, 256]
    for stage in range(3):
        steps = [
            Reduce(
                place, wires, LEAD_ORDERS[p][stage], dims[p], homes[p], outs[p], EVERY, lane[p],
                lead_gots[p * 3 + stage],
            )
            for p in range(2)
        ]
        for step in steps:
            step.begin()
        for step in steps:
            step.follow()
        if stage == 0:
            start_fetch(2)
            lead_block(0)
            lead_block(1)
        else:
            terms(5 * stage, 5 * stage + 2)
        for step in steps:
            step.relay()
        if stage == 0:
            terms(2, 5)
        else:
            terms(5 * stage + 2, 5 * stage + 5)
        for p, step in enumerate(steps):
            if stage < 2:
                acc = lead_sums[p * 2 + stage]

                def store(index, half, value, acc=acc):
                    acc[index + (EVERY, pl.ds(half * 128, 128))] = value

                homes[p] = outs[p] = acc
                lane[p] = 0
            else:
                at = [position(axis, place) for axis in LEAD_ORDERS[p]]
                rows = pl.ds(pl.multiple_of((at[0] * 16 + at[1] * 4 + at[2]) * 16, 16), 16)

                def store(index, half, value, p=p, rows=rows):
                    begin = pl.multiple_of(p * 512 + core * 256 + half * 128, 128)
                    work[rows, pl.ds(begin, 128)] = value

            step.finish(store)
            dims[p] = step.rest
    def gather_rows():
        slots = [2 * ((y + d) % 4) + core for d in range(4)]
        up, down = along("y", (y + 1) % 4, place), along("y", (y + 3) % 4, place)
        base = wires.take(8)

        def go(number, slot, lanes, dev):
            block = rows_t.at[pl.ds(pl.multiple_of(slot * 128, 128), 128), lanes]
            return wires.send(base + number, block, block, dev)

        whole, low, high = pl.ds(0, 512), pl.ds(0, 256), pl.ds(256, 256)
        one, two = go(0, slots[0], whole, up), go(1, slots[0], whole, down)
        passed = [go(4, slots[0], whole, mate)]
        yield
        one.wait_recv()
        three = go(2, slots[3], low, up)
        passed += [go(5, slots[3], whole, mate)]
        two.wait_recv()
        four = go(3, slots[1], high, down)
        passed += [go(6, slots[1], whole, mate)]
        yield
        three.wait_recv()
        four.wait_recv()
        passed += [go(7, slots[2], whole, mate)]
        for copy in passed:
            copy.wait_recv()
        for copy in passed + [one, two, three, four]:
            copy.wait_send()

    def all_rows():
        dims, rows = [DIMS] * 3, [pl.ds(begin, size) for begin, size in PARTS]
        homes, outs = [home] * 3, [out] * 3
        for stage in range(3):
            steps = [
                Reduce(
                    place, wires, ORDERS[p][stage], dims[p], homes[p], outs[p], rows[p], 0,
                    gots[p * 3 + stage],
                )
                for p in range(3)
            ]
            for step in steps:
                step.begin()
            if stage == 0:
                yield
            for step in steps:
                step.follow()
            yield
            for step in steps:
                step.relay()
            yield
            for p, step in enumerate(steps):
                if stage < 2:
                    acc = sums[p * 2 + stage]

                    def store(index, half, value, acc=acc):
                        acc[index + (EVERY, pl.ds(half * 128, 128))] = value

                    homes[p] = outs[p] = acc
                    rows[p] = EVERY
                else:

                    def store(index, half, value, p=p):
                        total[pl.ds(*PARTS[p]), pl.ds(half * 128, 128)] = value

                step.finish(store)
                dims[p] = step.rest
        mine = pl.ds(pl.multiple_of(core * 128, 128), 128)
        theirs = pl.ds(pl.multiple_of((1 - core) * 128, 128), 128)
        lanes = pl.ds(pl.multiple_of(core * 256, 256), 256)
        swapped = wires.send(wires.take(), total.at[theirs, :], tile.at[:, lanes], mate)
        tile[:, lanes] = total[mine, :]
        yield
        swapped.wait()
        rows_t[pl.ds(pl.multiple_of(gy * 128, 128), 128), :] = tile[...]
        yield from gather_rows()

    events = all_rows()

    for stage in range(3):
        steps = []
        for p in range(2):
            at = [position(axis, place) for axis in LEAD_ORDERS[p]]
            base = (at[0] * 256 + at[1] * 64, at[0] * 256, 0)[stage]
            begin = pl.multiple_of(p * 512 + core * 256, 256)
            halves = [pl.ds(begin, 128), pl.ds(pl.multiple_of(begin + 128, 128), 128)]
            steps.append(
                Gather(
                    place, wires, LEAD_ORDERS[p][2 - stage], work, base, (16, 64, 256)[stage],
                    pl.ds(begin, 256), halves, mate if stage == 2 else None,
                )
            )
        for step in steps:
            step.begin()
        if stage == 0:
            terms(15, 16)
        for _ in range(AHEAD[2 * stage]):
            next(events)
        for step in steps:
            step.relay()
        for _ in range(AHEAD[2 * stage + 1]):
            next(events)
        if stage < 2:
            for step in steps:
                step.arrive()
                step.finish()

    for step in steps:
        step.arrive()
    for step in steps:
        step.finish()
    for b in range(0, COLS, NB):
        block = work[b : b + NB, b : b + NB]
        work[b : b + NB, b : b + NB] = 0.5 * (block + block.T)
    count = [0]

    def between(_):
        if count[0] in WHEN:
            next(events)
        count[0] += 1

    invert_factor(work, a_ref, x_ref, between)
    for _ in events:
        pass
    block = work[pl.ds(pl.multiple_of(gy * 128, 128), 128), :]
    lane = lax.broadcasted_iota(jnp.int32, block.shape, 1)
    block = jnp.where(lane < (gy + 1) * 128, block, 0.0)
    mine = dot_two(block, rows_t[...])
    column = gy * 128 + lax.broadcasted_iota(jnp.int32, mine.shape, 0)
    row = (gx * 2 + gz) * 512 + lax.broadcasted_iota(jnp.int32, mine.shape, 1)
    factor[...] = jnp.where(column <= row, mine, 0.0).T


AHEAD = (1, 0, 1, 0, 0, 1)
WHEN = (35, 55, 74, 98, 110, 126)
WIRES = 180


def project(basis, cond, ground):
    any_spec = pl.BlockSpec(memory_space=pltpu.HBM)
    vmem = pl.BlockSpec(memory_space=pltpu.VMEM)
    lead_gots, lead_sums, gots, sums = [], [], [], []
    for _ in range(2):
        lead_gots += [
            pltpu.VMEM((6, 4, 4, 16, 128), BF16),
            pltpu.VMEM((6, 4, 16, 128), F32),
            pltpu.VMEM((6, 16, 128), F32),
        ]
        lead_sums += [pltpu.VMEM((4, 4, 16, 256), F32), pltpu.VMEM((4, 16, 256), F32)]
    for _, size in PARTS:
        gots += [
            pltpu.VMEM((6, 4, 4, size, 128), BF16),
            pltpu.VMEM((6, 4, size, 128), F32),
            pltpu.VMEM((6, size, 128), F32),
        ]
        sums += [pltpu.VMEM((4, 4, size, 256), F32), pltpu.VMEM((4, size, 256), F32)]
    return pl.pallas_call(
        kernel,
        out_shape=(
            jax.ShapeDtypeStruct((128, 512), F32),
            jax.ShapeDtypeStruct((512, 128), F32),
            jax.ShapeDtypeStruct((512, 4096), BF16),
        ),
        in_specs=[any_spec, vmem, vmem],
        out_specs=(vmem, vmem, any_spec),
        scratch_shapes=[
            pltpu.VMEM((512, COLS), BF16),
            pltpu.VMEM((512, COLS), BF16),
            pltpu.VMEM((5, 64, COLS), BF16),
            pltpu.VMEM((5, 64, COLS), BF16),
            pltpu.VMEM((64, 128), F32),
            pltpu.VMEM((1024, COLS), BF16),
            pltpu.VMEM((COLS, 1024), BF16),
            pltpu.VMEM((1024, 512), BF16),
            pltpu.VMEM((4, 4, 4, 16, 512), F32),
            pltpu.VMEM((4, 4, 4, 16, 512), BF16),
            pltpu.VMEM((2, 1024, 256), BF16),
            pltpu.VMEM((4, 4, 4, 256, 256), F32),
            pltpu.VMEM((4, 4, 4, 256, 256), BF16),
            pltpu.VMEM((COLS, COLS), F32),
            pltpu.VMEM((128, 128), F32),
            pltpu.VMEM((128, 128), F32),
            pltpu.VMEM((256, 256), F32),
            pltpu.VMEM((COLS, 512), F32),
            *lead_gots,
            *lead_sums,
            *gots,
            *sums,
            pltpu.SemaphoreType.DMA((7,)),
            pltpu.SemaphoreType.DMA((WIRES,)),
            pltpu.SemaphoreType.DMA((WIRES,)),
        ],
        compiler_params=pltpu.CompilerParams(
            collective_id=0, has_side_effects=True, vmem_limit_bytes=67043328
        ),
        name="project",
    )(basis, cond, ground)


def local(basis, classes, cond_table, ground_table, port_cells, port_load):
    cells_x, cells_y, cells_z, width = basis.shape
    cells = cells_x * cells_y * cells_z
    place = [
        lax.axis_index(axis) * size + jnp.arange(size, dtype=jnp.int32)
        for axis, size in (("gx", cells_x), ("gy", cells_y), ("gz", cells_z))
    ]
    total_y, total_z = cells_y * lax.axis_size("gy"), cells_z * lax.axis_size("gz")
    flat_ids = (
        (place[0][:, None, None] * total_y + place[1][None, :, None]) * total_z
        + place[2][None, None, :]
    ).reshape(cells)
    flat_classes = classes.reshape(cells)
    onehot = (flat_classes[:, None] == jnp.arange(16, dtype=jnp.int32)).astype(F32)
    conduct = jnp.sum(onehot * cond_table, axis=1)
    grounds = jnp.sum(onehot * ground_table, axis=1)
    matches = flat_ids[:, None] == port_cells[None, :]
    grounds = grounds + jnp.sum(jnp.where(matches, port_load[None, :], 0.0), axis=1)
    cond = jnp.broadcast_to(conduct[:, None], (cells, 128))
    ground = jnp.broadcast_to(grounds[:, None], (cells, 128))
    flat = basis.reshape(cells, width)
    tile, factor, _ = project(flat, cond, ground)
    return tile.T, factor


def solution(mesh):
    placed = (P("gx", "gy", "gz", None), P("gx", "gy", "gz"), P(), P(), P(), P())
    return jax.shard_map(
        local,
        mesh=mesh,
        in_specs=placed,
        out_specs=(P(("gx", "gz"), "gy"), P(("gx", "gz"), "gy")),
        check_vma=False,
    )
```

profile of v0, /device:TPU:1, one launch (start us, length us, event | category | flops | bytes accessed | tf_op | source)
XLA Modules:
  0.0 150.7 jit_solution(14519490978049756151)
XLA Ops:
  0.7 0.8 eq.28
  1.5 0.8 select_reduce_fusion.1
  2.3 0.1 add_multiply_fusion
  2.3 0.1 broadcast_add_fusion
  2.4 0.1 add.87
  2.5 1.3 select_reduce_fusion
  3.8 0.8 broadcast_in_dim.19.ground
  4.6 0.8 broadcast_in_dim.16.cond
  5.5 141.8 %project.1 = (f32[128,512]{1,0:T(8,128)}, f32[512,128]{1,0:T(8,128)}, bf16[512,4096]{1,0:T(8,128)(2,1)}) custom-call(bf16[512,8192]{1,0:T(8,128)(2,1)} %bitcast.2, f32[512,128]{1,0:T(8,128)} %broadcast_in_dim.16.cond, f32[512,128]{1,0:T(8,128)} %broadcast_in_dim.19.ground), custom_call_target="tpu_custom_call" | custom-call | tf_op jit(solution)/shard_map/project/pallas_call | solution.py:718
  147.3 1.8 %copy.9 = f32[512,128]{1,0:T(8,128)} copy(f32[512,128]{0,1:T(8,128)} %bitcast.3) | data formatting | bytes 524288
  149.1 1.7 %copy.11 = f32[512,128]{1,0:T(8,128)} copy(f32[512,128]{1,0:T(8,128)} %get-tuple-element.17) | data formatting | bytes 524288
  (3 shorter events, 0.0 us)
where the time goes:
time: 151 us
  Pallas kernels  142 us (94%)
  local copies, waits for them, and re-layouts  6.07 us (4%)
  other arithmetic  2.19 us (1%)
    pallas_call x1, Pallas kernels, project(): pl.pallas_call(kernel, out_shape=(jax.ShapeDtypeStruct((128, 512), F32),...  142 us
    unnamed x2, local copies, waits for them, and re-layouts  3.45 us

commit v1 on v0

--- a/solution.py
+++ b/solution.py
@@ -154,7 +154,7 @@
     def __init__(self, place, wires, axis, ref, base, size, lanes, halves, mate=None):
         self.ref, self.base, self.size, self.mate = ref, base, size, mate
         self.lanes, self.halves = lanes, halves
-        self.wires, self.first = wires, wires.take(8)
+        self.wires, self.first = wires, wires.take(10)
         me = position(axis, place)
         self.me, self.plus, self.minus, self.opposite = me, (me + 1) % 4, (me + 3) % 4, (me + 2) % 4
         self.up, self.down = along(axis, self.plus, place), along(axis, self.minus, place)
@@ -171,21 +171,27 @@
             self.passed.append(self.go(slot, pos, self.lanes, self.mate))
 
     def begin(self):
-        self.copies += [self.go(0, self.me, self.lanes, self.up)]
-        self.copies += [self.go(1, self.me, self.lanes, self.down)]
+        low, high = self.halves
+        self.copies += [self.go(0, self.me, low, self.up), self.go(1, self.me, high, self.down)]
+        self.copies += [self.go(8, self.me, high, self.up), self.go(9, self.me, low, self.down)]
         self.share(4, self.me)
 
     def relay(self):
+        low, high = self.halves
         self.copies[0].wait_recv()
-        self.copies += [self.go(2, self.minus, self.halves[0], self.up)]
+        self.copies += [self.go(2, self.minus, low, self.up)]
         self.copies[1].wait_recv()
-        self.copies += [self.go(3, self.plus, self.halves[1], self.down)]
+        self.copies += [self.go(3, self.plus, high, self.down)]
+
+    def pass_on(self):
+        self.copies[2].wait_recv()
+        self.copies[3].wait_recv()
         self.share(5, self.minus)
         self.share(6, self.plus)
 
     def arrive(self):
-        self.copies[2].wait_recv()
-        self.copies[3].wait_recv()
+        self.copies[4].wait_recv()
+        self.copies[5].wait_recv()
         self.share(7, self.opposite)
 
     def finish(self):
@@ -312,8 +318,8 @@
 
 
 def kernel(
-    basis, cond, ground, tile, factor, other,
-    panel, scaled, faces, halos, hz, image, image_t,
+    basis, classes, cond_table, ground_table, port_cells, port_load, tile, factor, other,
+    cond, ground, panel, scaled, faces, halos, hz, image, image_t,
     lead_window, lead_home, lead_out, window, home, out, work, a_ref, x_ref, total, rows_t,
     *rest,
 ):
@@ -360,6 +366,25 @@
     ]
     for copy in lead_swaps:
         copy.start()
+
+    def look_up(i, _):
+        kinds = classes[i]
+        lane = lax.broadcasted_iota(jnp.int32, (8, 8), 1)
+        diagonal = lane == lax.broadcasted_iota(jnp.int32, (8, 8), 0)
+        for table, out_ref in ((cond_table, cond), (ground_table, ground)):
+            values = jnp.zeros((8, 8), F32)
+            for kind in range(16):
+                values = jnp.where(kinds == kind, table[kind], values)
+            columns = []
+            for j in range(8):
+                line = jnp.broadcast_to(values[j : j + 1, :], (8, 8))
+                line = jnp.sum(jnp.where(diagonal, line, 0.0), axis=1, keepdims=True)
+                columns.append(jnp.broadcast_to(line, (8, 128)))
+            rows = pl.ds(pl.multiple_of(i * 64, 64), 64)
+            out_ref[rows, :] = jnp.concatenate(columns, axis=0)
+        return 0
+
+    lax.fori_loop(0, 8, look_up, 0)
     load.wait()
 
     def scale(c, _):
@@ -400,6 +425,18 @@
         return 0
 
     lax.fori_loop(2, 16, start_swap, 0)
+    def add_ports(i, _):
+        row = lax.broadcasted_iota(jnp.int32, (64, 128), 0)
+        flat = ((gx * 8 + i) * 64 + gy * 8 + row // 8) * 16 + gz * 8 + row % 8
+        found = jnp.zeros((64, 128), F32)
+        for j in range(16):
+            match = flat == jnp.broadcast_to(port_cells[j : j + 1, :], (64, 128))
+            found = found + jnp.where(match, jnp.broadcast_to(port_load[j : j + 1, :], (64, 128)), 0.0)
+        rows = pl.ds(pl.multiple_of(i * 64, 64), 64)
+        ground[rows, :] = ground[rows, :] + jnp.sum(found, axis=1, keepdims=True)
+        return 0
+
+    lax.fori_loop(0, 8, add_ports, 0)
     for copy in face_copies:
         copy.wait()
 
@@ -564,29 +601,32 @@
     def gather_rows():
         slots = [2 * ((y + d) % 4) + core for d in range(4)]
         up, down = along("y", (y + 1) % 4, place), along("y", (y + 3) % 4, place)
-        base = wires.take(8)
+        base = wires.take(10)
 
         def go(number, slot, lanes, dev):
             block = rows_t.at[pl.ds(pl.multiple_of(slot * 128, 128), 128), lanes]
             return wires.send(base + number, block, block, dev)
 
         whole, low, high = pl.ds(0, 512), pl.ds(0, 256), pl.ds(256, 256)
-        one, two = go(0, slots[0], whole, up), go(1, slots[0], whole, down)
+        one, two = go(0, slots[0], low, up), go(1, slots[0], high, down)
+        three, four = go(8, slots[0], high, up), go(9, slots[0], low, down)
         passed = [go(4, slots[0], whole, mate)]
         yield
         one.wait_recv()
-        three = go(2, slots[3], low, up)
-        passed += [go(5, slots[3], whole, mate)]
+        five = go(2, slots[3], low, up)
         two.wait_recv()
-        four = go(3, slots[1], high, down)
-        passed += [go(6, slots[1], whole, mate)]
+        six = go(3, slots[1], high, down)
         yield
         three.wait_recv()
+        passed += [go(5, slots[3], whole, mate)]
         four.wait_recv()
+        passed += [go(6, slots[1], whole, mate)]
+        five.wait_recv()
+        six.wait_recv()
         passed += [go(7, slots[2], whole, mate)]
         for copy in passed:
             copy.wait_recv()
-        for copy in passed + [one, two, three, four]:
+        for copy in passed + [one, two, three, four, five, six]:
             copy.wait_send()
 
     def all_rows():
@@ -659,6 +699,8 @@
             next(events)
         for step in steps:
             step.relay()
+        for step in steps:
+            step.pass_on()
         for _ in range(AHEAD[2 * stage + 1]):
             next(events)
         if stage < 2:
@@ -689,17 +731,18 @@
     mine = dot_two(block, rows_t[...])
     column = gy * 128 + lax.broadcasted_iota(jnp.int32, mine.shape, 0)
     row = (gx * 2 + gz) * 512 + lax.broadcasted_iota(jnp.int32, mine.shape, 1)
-    factor[...] = jnp.where(column <= row, mine, 0.0).T
+    factor[...] = jnp.where(column <= row, mine, 0.0)
 
 
 AHEAD = (1, 0, 1, 0, 0, 1)
-WHEN = (35, 55, 74, 98, 110, 126)
-WIRES = 180
-
-
-def project(basis, cond, ground):
+WHEN = (35, 55, 80, 94, 104, 111, 128)
+WIRES = 200
+
+
+def project(basis, classes, cond_table, ground_table, port_cells, port_load):
     any_spec = pl.BlockSpec(memory_space=pltpu.HBM)
     vmem = pl.BlockSpec(memory_space=pltpu.VMEM)
+    smem = pl.BlockSpec(memory_space=pltpu.SMEM)
     lead_gots, lead_sums, gots, sums = [], [], [], []
     for _ in range(2):
         lead_gots += [
@@ -719,12 +762,14 @@
         kernel,
         out_shape=(
             jax.ShapeDtypeStruct((128, 512), F32),
-            jax.ShapeDtypeStruct((512, 128), F32),
+            jax.ShapeDtypeStruct((128, 512), F32),
             jax.ShapeDtypeStruct((512, 4096), BF16),
         ),
-        in_specs=[any_spec, vmem, vmem],
+        in_specs=[any_spec, vmem, smem, smem, vmem, vmem],
         out_specs=(vmem, vmem, any_spec),
         scratch_shapes=[
+            pltpu.VMEM((512, 128), F32),
+            pltpu.VMEM((512, 128), F32),
             pltpu.VMEM((512, COLS), BF16),
             pltpu.VMEM((512, COLS), BF16),
             pltpu.VMEM((5, 64, COLS), BF16),
@@ -755,32 +800,21 @@
             collective_id=0, has_side_effects=True, vmem_limit_bytes=67043328
         ),
         name="project",
-    )(basis, cond, ground)
+    )(basis, classes, cond_table, ground_table, port_cells, port_load)
+
+
+def turn_kernel(tile, factor, tile_out, factor_out):
+    tile_out[...] = tile[...].T
+    factor_out[...] = factor[...].T
 
 
 def local(basis, classes, cond_table, ground_table, port_cells, port_load):
-    cells_x, cells_y, cells_z, width = basis.shape
-    cells = cells_x * cells_y * cells_z
-    place = [
-        lax.axis_index(axis) * size + jnp.arange(size, dtype=jnp.int32)
-        for axis, size in (("gx", cells_x), ("gy", cells_y), ("gz", cells_z))
-    ]
-    total_y, total_z = cells_y * lax.axis_size("gy"), cells_z * lax.axis_size("gz")
-    flat_ids = (
-        (place[0][:, None, None] * total_y + place[1][None, :, None]) * total_z
-        + place[2][None, None, :]
-    ).reshape(cells)
-    flat_classes = classes.reshape(cells)
-    onehot = (flat_classes[:, None] == jnp.arange(16, dtype=jnp.int32)).astype(F32)
-    conduct = jnp.sum(onehot * cond_table, axis=1)
-    grounds = jnp.sum(onehot * ground_table, axis=1)
-    matches = flat_ids[:, None] == port_cells[None, :]
-    grounds = grounds + jnp.sum(jnp.where(matches, port_load[None, :], 0.0), axis=1)
-    cond = jnp.broadcast_to(conduct[:, None], (cells, 128))
-    ground = jnp.broadcast_to(grounds[:, None], (cells, 128))
-    flat = basis.reshape(cells, width)
-    tile, factor, _ = project(flat, cond, ground)
-    return tile.T, factor
+    flat = basis.reshape(512, basis.shape[3])
+    tile, factor, _ = project(
+        flat, classes, cond_table, ground_table, port_cells.reshape(16, 128), port_load.reshape(16, 128)
+    )
+    shape = jax.ShapeDtypeStruct((512, 128), F32)
+    return pl.pallas_call(turn_kernel, out_shape=(shape, shape), name="turn")(tile, factor)
 
 
 def solution(mesh):

time: 151 us -> 138 us (0.914)
  local copies, waits for them, and re-layouts: 6.07 us -> 0 us
  Pallas kernels: 142 us -> 137 us
  other arithmetic: 2.19 us -> 0 us
    pallas_call x1, Pallas kernels: 142 us -> 135 us  [project(): pl.pallas_call(kernel, out_shape=(jax.ShapeDtypeStruct((128, 512), F32),...]
    unnamed x2 -> x0, local copies, waits for them, and re-layouts: 3.45 us -> none
    reduce_sum x2 -> x0, other arithmetic: 2.03 us -> none  [the longest x1 1.27 us: local(): jnp.sum(jnp.where(matches, port_load[None, :], 0.0), axis=1)]
    pallas_call x0 -> x1, Pallas kernels: none -> 1.95 us  [local(): pl.pallas_call(turn_kernel, out_shape=(shape, shape), name='turn')]
    broadcast_in_dim x2 -> x0, local copies, waits for them, and re-layouts: 1.68 us -> none  [the longest x1 0.84 us: local(): ground = jnp.broadcast_to(grounds[:, None], (cells, 128))]
where the time goes in v1:
time: 138 us
  Pallas kernels  137 us (99%)
    pallas_call x1, Pallas kernels, project(): pl.pallas_call(kernel, out_shape=(jax.ShapeDtypeStruct((128, 512), F32),...  135 us

profile of v1, /device:TPU:1, one launch (start us, length us, event | category | flops | bytes accessed | tf_op | source)
XLA Modules:
  0.0 137.5 jit_solution(10985726870969192424)
XLA Ops:
  0.6 134.9 %project.1 = (f32[128,512]{1,0:T(8,128)}, f32[128,512]{1,0:T(8,128)}, bf16[512,4096]{1,0:T(8,128)(2,1)}) custom-call(bf16[512,8192]{1,0:T(8,128)(2,1)} %bitcast.3, s32[8,8,8]{2,1,0:T(8,128)} %classes.1, f32[16]{0:T(128)} %cond_table.1, f32[16]{0:T(128)} %ground_table.1, s32[16,128]{1,0:T(8,128)} %bitcast.4, f32[16,128]{1,0:T(8,128)} %bitcast.5), custom_call_target="tpu_custom_call" | custom-call | tf_op jit(solution)/shard_map/project/pallas_call | solution.py:761
  135.6 2.0 %turn.1 = (f32[512,128]{1,0:T(8,128)}, f32[512,128]{1,0:T(8,128)}) custom-call(f32[128,512]{1,0:T(8,128)} %get-tuple-element.4.tile, f32[128,512]{1,0:T(8,128)} %get-tuple-element.5.factor), custom_call_target="tpu_custom_call" | custom-call | tf_op jit(solution)/shard_map/turn/pallas_call | solution.py:817

commit v2 on v1

--- a/solution.py
+++ b/solution.py
@@ -11,6 +11,7 @@
 F32 = jnp.float32
 BF16 = jnp.bfloat16
 MESH = pl.DeviceIdType.MESH
+EVERY = slice(None)
 
 
 def here():
@@ -49,7 +50,7 @@
     peers = []
     for axis in "xyz":
         pos = position(axis, place)
-        peers += [along(axis, (pos + 1) % 4, place), along(axis, (pos + 3) % 4, place)]
+        peers += [along(axis, (pos + d) % 4, place) for d in (1, 2, 3)]
     return peers + [device(x, y, z, 1 - core)]
 
 
@@ -77,17 +78,16 @@
         return copy
 
 
-def each(dims, body):
-    count = 4 ** len(dims)
-    if count == 1:
-        body(())
+def each(dims, body, loop):
+    if not loop or len(dims) < 2:
+        body((EVERY,) * len(dims))
         return
 
     def step(i, _):
-        body(tuple((i // 4 ** (len(dims) - 1 - d)) % 4 for d in range(len(dims))))
+        body((i,) + (EVERY,) * (len(dims) - 1))
         return 0
 
-    lax.fori_loop(0, count, step, 0)
+    lax.fori_loop(0, 4, step, 0)
 
 
 def put(index, dims, axis, pos):
@@ -97,8 +97,12 @@
 
 
 class Reduce:
-    def __init__(self, place, wires, axis, dims, home, out, rows, lane, got):
+    def __init__(
+        self, place, wires, axis, dims, home, out, rows, lane, got, loop=False, direct=False
+    ):
         self.axis, self.dims, self.home, self.out, self.rows, self.got = axis, dims, home, out, rows, got
+        self.loop, self.direct = loop, direct
+        self.across = along(axis, (position(axis, place) + 2) % 4, place)
         self.first, self.second = pl.ds(lane, 128), pl.ds(lane + 128, 128)
         self.rest = tuple(d for d in dims if d != axis)
         self.wires, self.base = wires, wires.take(6)
@@ -113,14 +117,19 @@
         self.copies[slot] = self.wires.send(self.base + slot, src, self.got.at[slot], dev)
 
     def begin(self):
-        self.go(0, self.opposite, self.first, self.up)
-        self.go(3, self.opposite, self.second, self.down)
+        self.go(0, self.opposite, self.first, self.across if self.direct else self.up)
+        self.go(3, self.opposite, self.second, self.across if self.direct else self.down)
 
     def follow(self):
         self.go(1, self.plus, self.second, self.up)
         self.go(4, self.minus, self.first, self.down)
+        if self.direct:
+            self.go(2, self.plus, self.first, self.up)
+            self.go(5, self.minus, self.second, self.down)
 
     def relay(self):
+        if self.direct:
+            return
         for slot, pos, lanes, dev in (
             (0, self.plus, self.first, self.up),
             (3, self.minus, self.second, self.down),
@@ -132,20 +141,23 @@
                 total = self.home[at] + self.got[(slot,) + index].astype(F32)
                 self.out[at] = total.astype(self.out.dtype)
 
-            each(self.rest, body)
+            each(self.rest, body, self.loop)
             self.go(slot + 2, pos, lanes, dev)
 
     def finish(self, store):
-        for slot in (1, 4, 2, 5):
+        for slot in (1, 4, 2, 5) + ((0, 3) if self.direct else ()):
             self.copies[slot].wait_recv()
 
         def body(index):
             for half, lanes, one, two in ((0, self.first, 2, 4), (1, self.second, 1, 5)):
                 at = put(index, self.dims, self.axis, self.me) + (self.rows, lanes)
                 total = self.home[at] + self.got[(one,) + index].astype(F32)
-                store(index, half, total + self.got[(two,) + index].astype(F32))
-
-        each(self.rest, body)
+                total = total + self.got[(two,) + index].astype(F32)
+                if self.direct:
+                    total = total + self.got[(3 * half,) + index].astype(F32)
+                store(index, half, total)
+
+        each(self.rest, body, self.loop)
         for copy in self.copies.values():
             copy.wait_send()
 
@@ -158,6 +170,7 @@
         me = position(axis, place)
         self.me, self.plus, self.minus, self.opposite = me, (me + 1) % 4, (me + 3) % 4, (me + 2) % 4
         self.up, self.down = along(axis, self.plus, place), along(axis, self.minus, place)
+        self.across = along(axis, self.opposite, place)
         self.copies = []
         self.passed = []
 
@@ -171,12 +184,18 @@
             self.passed.append(self.go(slot, pos, self.lanes, self.mate))
 
     def begin(self):
+        if self.mate is None:
+            for slot, dev in enumerate((self.across, self.up, self.down)):
+                self.copies += [self.go(slot, self.me, self.lanes, dev)]
+            return
         low, high = self.halves
         self.copies += [self.go(0, self.me, low, self.up), self.go(1, self.me, high, self.down)]
         self.copies += [self.go(8, self.me, high, self.up), self.go(9, self.me, low, self.down)]
         self.share(4, self.me)
 
     def relay(self):
+        if self.mate is None:
+            return
         low, high = self.halves
         self.copies[0].wait_recv()
         self.copies += [self.go(2, self.minus, low, self.up)]
@@ -184,12 +203,18 @@
         self.copies += [self.go(3, self.plus, high, self.down)]
 
     def pass_on(self):
+        if self.mate is None:
+            return
         self.copies[2].wait_recv()
         self.copies[3].wait_recv()
         self.share(5, self.minus)
         self.share(6, self.plus)
 
     def arrive(self):
+        if self.mate is None:
+            for copy in self.copies:
+                copy.wait_recv()
+            return
         self.copies[4].wait_recv()
         self.copies[5].wait_recv()
         self.share(7, self.opposite)
@@ -313,7 +338,6 @@
 ORDERS = ("xyz", "yzx", "zxy")
 LEAD_ORDERS = ("xyz", "yzx")
 PARTS = ((0, 96), (96, 80), (176, 80))
-EVERY = slice(None)
 CHUNKS = COLS // 128
 
 
@@ -559,7 +583,7 @@
         steps = [
             Reduce(
                 place, wires, LEAD_ORDERS[p][stage], dims[p], homes[p], outs[p], EVERY, lane[p],
-                lead_gots[p * 3 + stage],
+                lead_gots[p * 3 + stage], direct=stage > 0,
             )
             for p in range(2)
         ]
@@ -636,7 +660,7 @@
             steps = [
                 Reduce(
                     place, wires, ORDERS[p][stage], dims[p], homes[p], outs[p], rows[p], 0,
-                    gots[p * 3 + stage],
+                    gots[p * 3 + stage], loop=True, direct=stage == 2,
                 )
                 for p in range(3)
             ]
@@ -647,9 +671,10 @@
             for step in steps:
                 step.follow()
             yield
-            for step in steps:
-                step.relay()
-            yield
+            if stage < 2:
+                for step in steps:
+                    step.relay()
+                yield
             for p, step in enumerate(steps):
                 if stage < 2:
                     acc = sums[p * 2 + stage]
@@ -735,7 +760,7 @@
 
 
 AHEAD = (1, 0, 1, 0, 0, 1)
-WHEN = (35, 55, 80, 94, 104, 111, 128)
+WHEN = (34, 55, 80, 98, 105, 122)
 WIRES = 200
 
 

time: 138 us -> 130 us (0.942)
  Pallas kernels: 137 us -> 130 us
    pallas_call x1, Pallas kernels: 135 us -> 128 us  [project(): pl.pallas_call(kernel, out_shape=(jax.ShapeDtypeStruct((128, 512), F32),...]
where the time goes in v2:
time: 130 us
  Pallas kernels  130 us (100%)
    pallas_call x1, Pallas kernels, project(): pl.pallas_call(kernel, out_shape=(jax.ShapeDtypeStruct((128, 512), F32),...  128 us

profile of v2, /device:TPU:1, one launch (start us, length us, event | category | flops | bytes accessed | tf_op | source)
XLA Modules:
  0.0 130.2 jit_solution(7371745996045919111)
XLA Ops:
  0.6 127.6 %project.1 = (f32[128,512]{1,0:T(8,128)}, f32[128,512]{1,0:T(8,128)}, bf16[512,4096]{1,0:T(8,128)(2,1)}) custom-call(bf16[512,8192]{1,0:T(8,128)(2,1)} %bitcast.3, s32[8,8,8]{2,1,0:T(8,128)} %classes.1, f32[16]{0:T(128)} %cond_table.1, f32[16]{0:T(128)} %ground_table.1, s32[16,128]{1,0:T(8,128)} %bitcast.4, f32[16,128]{1,0:T(8,128)} %bitcast.5), custom_call_target="tpu_custom_call" | custom-call | tf_op jit(solution)/shard_map/project/pallas_call | solution.py:786
  128.3 2.0 %turn.1 = (f32[512,128]{1,0:T(8,128)}, f32[512,128]{1,0:T(8,128)}) custom-call(f32[128,512]{1,0:T(8,128)} %get-tuple-element.4.tile, f32[128,512]{1,0:T(8,128)} %get-tuple-element.5.factor), custom_call_target="tpu_custom_call" | custom-call | tf_op jit(solution)/shard_map/turn/pallas_call | solution.py:842

commit v3 on v2

--- a/solution.py
+++ b/solution.py
@@ -163,7 +163,7 @@
 
 
 class Gather:
-    def __init__(self, place, wires, axis, ref, base, size, lanes, halves, mate=None):
+    def __init__(self, place, wires, axis, ref, base, size, lanes, halves, mate=None, relayed=False):
         self.ref, self.base, self.size, self.mate = ref, base, size, mate
         self.lanes, self.halves = lanes, halves
         self.wires, self.first = wires, wires.take(10)
@@ -171,6 +171,7 @@
         self.me, self.plus, self.minus, self.opposite = me, (me + 1) % 4, (me + 3) % 4, (me + 2) % 4
         self.up, self.down = along(axis, self.plus, place), along(axis, self.minus, place)
         self.across = along(axis, self.opposite, place)
+        self.direct = mate is None and not relayed
         self.copies = []
         self.passed = []
 
@@ -184,7 +185,7 @@
             self.passed.append(self.go(slot, pos, self.lanes, self.mate))
 
     def begin(self):
-        if self.mate is None:
+        if self.direct:
             for slot, dev in enumerate((self.across, self.up, self.down)):
                 self.copies += [self.go(slot, self.me, self.lanes, dev)]
             return
@@ -194,7 +195,7 @@
         self.share(4, self.me)
 
     def relay(self):
-        if self.mate is None:
+        if self.direct:
             return
         low, high = self.halves
         self.copies[0].wait_recv()
@@ -203,7 +204,7 @@
         self.copies += [self.go(3, self.plus, high, self.down)]
 
     def pass_on(self):
-        if self.mate is None:
+        if self.direct:
             return
         self.copies[2].wait_recv()
         self.copies[3].wait_recv()
@@ -211,7 +212,7 @@
         self.share(6, self.plus)
 
     def arrive(self):
-        if self.mate is None:
+        if self.direct:
             for copy in self.copies:
                 copy.wait_recv()
             return
@@ -623,35 +624,20 @@
             step.finish(store)
             dims[p] = step.rest
     def gather_rows():
-        slots = [2 * ((y + d) % 4) + core for d in range(4)]
-        up, down = along("y", (y + 1) % 4, place), along("y", (y + 3) % 4, place)
-        base = wires.take(10)
-
-        def go(number, slot, lanes, dev):
-            block = rows_t.at[pl.ds(pl.multiple_of(slot * 128, 128), 128), lanes]
-            return wires.send(base + number, block, block, dev)
-
-        whole, low, high = pl.ds(0, 512), pl.ds(0, 256), pl.ds(256, 256)
-        one, two = go(0, slots[0], low, up), go(1, slots[0], high, down)
-        three, four = go(8, slots[0], high, up), go(9, slots[0], low, down)
-        passed = [go(4, slots[0], whole, mate)]
+        step = Gather(
+            place, wires, "y", rows_t, 0, 256, pl.ds(0, 256), [pl.ds(0, 128), pl.ds(128, 128)], relayed=True
+        )
+        step.begin()
         yield
-        one.wait_recv()
-        five = go(2, slots[3], low, up)
-        two.wait_recv()
-        six = go(3, slots[1], high, down)
+        step.relay()
         yield
-        three.wait_recv()
-        passed += [go(5, slots[3], whole, mate)]
-        four.wait_recv()
-        passed += [go(6, slots[1], whole, mate)]
-        five.wait_recv()
-        six.wait_recv()
-        passed += [go(7, slots[2], whole, mate)]
-        for copy in passed:
-            copy.wait_recv()
-        for copy in passed + [one, two, three, four, five, six]:
-            copy.wait_send()
+        step.pass_on()
+        step.arrive()
+        step.finish()
+
+    mine = pl.ds(pl.multiple_of(gy * 128, 128), 128)
+    theirs = pl.ds(pl.multiple_of((gy + 1 - 2 * core) * 128, 128), 128)
+    lanes = pl.ds(pl.multiple_of(core * 256, 256), 256)
 
     def all_rows():
         dims, rows = [DIMS] * 3, [pl.ds(begin, size) for begin, size in PARTS]
@@ -687,19 +673,15 @@
                 else:
 
                     def store(index, half, value, p=p):
-                        total[pl.ds(*PARTS[p]), pl.ds(half * 128, 128)] = value
+                        begin = pl.multiple_of(y * 256 + PARTS[p][0], 16)
+                        rows_t[pl.ds(begin, PARTS[p][1]), pl.ds(half * 128, 128)] = value
 
                 step.finish(store)
                 dims[p] = step.rest
-        mine = pl.ds(pl.multiple_of(core * 128, 128), 128)
-        theirs = pl.ds(pl.multiple_of((1 - core) * 128, 128), 128)
-        lanes = pl.ds(pl.multiple_of(core * 256, 256), 256)
-        swapped = wires.send(wires.take(), total.at[theirs, :], tile.at[:, lanes], mate)
-        tile[:, lanes] = total[mine, :]
-        yield
+        swapped = wires.send(wires.take(), rows_t.at[theirs, :], tile.at[:, lanes], mate)
+        tile[:, lanes] = rows_t[mine, :]
+        yield from gather_rows()
         swapped.wait()
-        rows_t[pl.ds(pl.multiple_of(gy * 128, 128), 128), :] = tile[...]
-        yield from gather_rows()
 
     events = all_rows()
 
@@ -750,17 +732,25 @@
     invert_factor(work, a_ref, x_ref, between)
     for _ in events:
         pass
-    block = work[pl.ds(pl.multiple_of(gy * 128, 128), 128), :]
-    lane = lax.broadcasted_iota(jnp.int32, block.shape, 1)
-    block = jnp.where(lane < (gy + 1) * 128, block, 0.0)
-    mine = dot_two(block, rows_t[...])
-    column = gy * 128 + lax.broadcasted_iota(jnp.int32, mine.shape, 0)
-    row = (gx * 2 + gz) * 512 + lax.broadcasted_iota(jnp.int32, mine.shape, 1)
-    factor[...] = jnp.where(column <= row, mine, 0.0)
+    last = None
+    for columns, side in ((theirs, gy + 1 - 2 * core), (mine, gy)):
+        block = work[columns, :]
+        lane = lax.broadcasted_iota(jnp.int32, block.shape, 1)
+        block = jnp.where(lane < (side + 1) * 128, block, 0.0)
+        value = dot_two(block, rows_t[...])
+        column = side * 128 + lax.broadcasted_iota(jnp.int32, value.shape, 0)
+        row = (gx * 2 + gz) * 512 + core * 256 + lax.broadcasted_iota(jnp.int32, value.shape, 1)
+        value = jnp.where(column <= row, value, 0.0)
+        if last is None:
+            total[...] = value
+            last = wires.send(wires.take(), total, factor.at[:, lanes], mate)
+        else:
+            factor[:, lanes] = value
+    last.wait()
 
 
 AHEAD = (1, 0, 1, 0, 0, 1)
-WHEN = (34, 55, 80, 98, 105, 122)
+WHEN = (26, 46, 72, 90, 108)
 WIRES = 200
 
 
@@ -811,8 +801,8 @@
             pltpu.VMEM((COLS, COLS), F32),
             pltpu.VMEM((128, 128), F32),
             pltpu.VMEM((128, 128), F32),
-            pltpu.VMEM((256, 256), F32),
-            pltpu.VMEM((COLS, 512), F32),
+            pltpu.VMEM((128, 256), F32),
+            pltpu.VMEM((COLS, 256), F32),
             *lead_gots,
             *lead_sums,
             *gots,

time: 130 us -> 128 us (0.985)
  Pallas kernels: 130 us -> 127 us
    pallas_call x1, Pallas kernels: 128 us -> 125 us  [project(): pl.pallas_call(kernel, out_shape=(jax.ShapeDtypeStruct((128, 512), F32),...]
where the time goes in v3:
time: 128 us
  Pallas kernels  127 us (99%)
    pallas_call x1, Pallas kernels, project(): pl.pallas_call(kernel, out_shape=(jax.ShapeDtypeStruct((128, 512), F32),...  125 us

profile of v3, /device:TPU:1, one launch (start us, length us, event | category | flops | bytes accessed | tf_op | source)
XLA Modules:
  0.0 127.7 jit_solution(10588808191882368339)
XLA Ops:
  0.6 125.1 %project.1 = (f32[128,512]{1,0:T(8,128)}, f32[128,512]{1,0:T(8,128)}, bf16[512,4096]{1,0:T(8,128)(2,1)}) custom-call(bf16[512,8192]{1,0:T(8,128)(2,1)} %bitcast.3, s32[8,8,8]{2,1,0:T(8,128)} %classes.1, f32[16]{0:T(128)} %cond_table.1, f32[16]{0:T(128)} %ground_table.1, s32[16,128]{1,0:T(8,128)} %bitcast.4, f32[16,128]{1,0:T(8,128)} %bitcast.5), custom_call_target="tpu_custom_call" | custom-call | tf_op jit(solution)/shard_map/project/pallas_call | solution.py:776
  125.7 2.0 %turn.1 = (f32[512,128]{1,0:T(8,128)}, f32[512,128]{1,0:T(8,128)}) custom-call(f32[128,512]{1,0:T(8,128)} %get-tuple-element.4.tile, f32[128,512]{1,0:T(8,128)} %get-tuple-element.5.factor), custom_call_target="tpu_custom_call" | custom-call | tf_op jit(solution)/shard_map/turn/pallas_call | solution.py:832

commit v4 on v3

--- a/solution.py
+++ b/solution.py
@@ -145,6 +145,10 @@
             self.go(slot + 2, pos, lanes, dev)
 
     def finish(self, store):
+        self.collect(store)
+        self.drain()
+
+    def collect(self, store):
         for slot in (1, 4, 2, 5) + ((0, 3) if self.direct else ()):
             self.copies[slot].wait_recv()
 
@@ -158,6 +162,8 @@
                 store(index, half, total)
 
         each(self.rest, body, self.loop)
+
+    def drain(self):
         for copy in self.copies.values():
             copy.wait_send()
 
@@ -640,44 +646,45 @@
     lanes = pl.ds(pl.multiple_of(core * 256, 256), 256)
 
     def all_rows():
-        dims, rows = [DIMS] * 3, [pl.ds(begin, size) for begin, size in PARTS]
-        homes, outs = [home] * 3, [out] * 3
-        for stage in range(3):
-            steps = [
-                Reduce(
-                    place, wires, ORDERS[p][stage], dims[p], homes[p], outs[p], rows[p], 0,
-                    gots[p * 3 + stage], loop=True, direct=stage == 2,
-                )
-                for p in range(3)
-            ]
+        def make(p, stage, dims, terms_ref, sent_ref, rows):
+            return Reduce(
+                place, wires, ORDERS[p][stage], dims, terms_ref, sent_ref, rows, 0,
+                gots[p * 3 + stage], loop=True, direct=stage == 2,
+            )
+
+        steps = [make(p, 0, DIMS, home, out, pl.ds(*PARTS[p])) for p in range(3)]
+        for step in steps:
+            step.begin()
+        yield
+        for step in steps:
+            step.follow()
+        yield
+        for stage in range(2):
             for step in steps:
-                step.begin()
-            if stage == 0:
-                yield
+                step.relay()
+            yield
+            later = []
+            for p, step in enumerate(steps):
+                acc = sums[p * 2 + stage]
+
+                def store(index, half, value, acc=acc):
+                    acc[index + (EVERY, pl.ds(half * 128, 128))] = value
+
+                step.collect(store)
+                later.append(make(p, stage + 1, step.rest, acc, acc, EVERY))
+                later[p].begin()
+                later[p].follow()
             for step in steps:
-                step.follow()
+                step.drain()
+            steps = later
             yield
-            if stage < 2:
-                for step in steps:
-                    step.relay()
-                yield
-            for p, step in enumerate(steps):
-                if stage < 2:
-                    acc = sums[p * 2 + stage]
-
-                    def store(index, half, value, acc=acc):
-                        acc[index + (EVERY, pl.ds(half * 128, 128))] = value
-
-                    homes[p] = outs[p] = acc
-                    rows[p] = EVERY
-                else:
-
-                    def store(index, half, value, p=p):
-                        begin = pl.multiple_of(y * 256 + PARTS[p][0], 16)
-                        rows_t[pl.ds(begin, PARTS[p][1]), pl.ds(half * 128, 128)] = value
-
-                step.finish(store)
-                dims[p] = step.rest
+        for p, step in enumerate(steps):
+
+            def store(index, half, value, p=p):
+                begin = pl.multiple_of(y * 256 + PARTS[p][0], 16)
+                rows_t[pl.ds(begin, PARTS[p][1]), pl.ds(half * 128, 128)] = value
+
+            step.finish(store)
         swapped = wires.send(wires.take(), rows_t.at[theirs, :], tile.at[:, lanes], mate)
         tile[:, lanes] = rows_t[mine, :]
         yield from gather_rows()

time: 128 us -> 127 us (level)
  no operation moved by 1% of the time
where the time goes in v4:
time: 127 us
  Pallas kernels  126 us (99%)
    pallas_call x1, Pallas kernels, project(): pl.pallas_call(kernel, out_shape=(jax.ShapeDtypeStruct((128, 512), F32),...  124 us

profile of v4, /device:TPU:1, one launch (start us, length us, event | category | flops | bytes accessed | tf_op | source)
XLA Modules:
  0.0 127.0 jit_solution(12632758298606405407)
XLA Ops:
  0.6 124.4 %project.1 = (f32[128,512]{1,0:T(8,128)}, f32[128,512]{1,0:T(8,128)}, bf16[512,4096]{1,0:T(8,128)(2,1)}) custom-call(bf16[512,8192]{1,0:T(8,128)(2,1)} %bitcast.3, s32[8,8,8]{2,1,0:T(8,128)} %classes.1, f32[16]{0:T(128)} %cond_table.1, f32[16]{0:T(128)} %ground_table.1, s32[16,128]{1,0:T(8,128)} %bitcast.4, f32[16,128]{1,0:T(8,128)} %bitcast.5), custom_call_target="tpu_custom_call" | custom-call | tf_op jit(solution)/shard_map/project/pallas_call | solution.py:783
  125.0 2.0 %turn.1 = (f32[512,128]{1,0:T(8,128)}, f32[512,128]{1,0:T(8,128)}) custom-call(f32[128,512]{1,0:T(8,128)} %get-tuple-element.4.tile, f32[128,512]{1,0:T(8,128)} %get-tuple-element.5.factor), custom_call_target="tpu_custom_call" | custom-call | tf_op jit(solution)/shard_map/turn/pallas_call | solution.py:839
